TPU v7x, 1024 devices: a whole 4x4x32 slice. The times are simulated.
1024 devices in a mesh: dp: 4 (over y), section: 8 (over x, core), tensor: 32 (over z).
Axes of the slice: x: 4, y: 4, z: 32, core: 2. Of those that a mesh axis runs over, the one named last changes fastest.
Arguments:
- hidden: bfloat16 [8, 512, 8192], P('section', 'dp', 'tensor'), may hold values from -6 to 6
- q_weight: bfloat16 [8, 8192, 8192], P('section', None, 'tensor'), may hold values from -0.0625 to 0.0625
- o_weight: bfloat16 [8, 8192, 8192], P('section', 'tensor'), may hold values from -0.0625 to 0.0625
- vision_kv: bfloat16 [8, 8, 1024, 2048], P(None, None, ('dp', 'section', 'tensor')), may hold values from -6 to 6
- q_gain: float32 [8, 128], P('section'), may hold values from 1.5 to 8
- k_gain: float32 [8, 128], P('section'), may hold values from 1.5 to 8
- attn_gate: float32 [8], P('section'), may hold values from 0.25 to 1.5
- images: int32 [8], replicated, may hold values from 1 to 2
- tiles: int32 [8, 2], replicated, may hold values from 1 to 4
- text_start: int32 [8, 2], replicated, may hold values from 0 to 63
Outputs:
- layer_out: bfloat16 [8, 512, 8192], P('section', 'dp', 'tensor')
All inputs are finite; a program needn't handle non-finite values.
Results may differ from a plain program's by a relative error of at most 0.02.
Values may be sent and summed in bfloat16 or wider, within the bound.
A program may use at most 64 MiB of HBM per device.

v0:
```python
import jax
import jax.numpy as jnp
from jax import lax
from jax.sharding import PartitionSpec as P

TILES = 4
IMG = 2
P_SIZE = 128


def normalize(values, gain):
    mean_square = jnp.mean(values * values, axis=-1, keepdims=True)
    return values * lax.rsqrt(mean_square + 1e-05) * gain


def spread(block, kv_heads, n_tensor, head_dim):
    split = block.reshape(block.shape[:-1] + (kv_heads, 2 * head_dim))
    return jnp.repeat(split, n_tensor // kv_heads, axis=-2)


def on_device(
    hidden, q_weight, o_weight, vision_kv, q_gain, k_gain, attn_gate, images, tiles, text_start
):
    n_tensor = lax.axis_size("tensor")
    n_section = lax.axis_size("section")
    n_replica = lax.axis_size("dp")
    head_dim = q_gain.shape[1]
    heads_dev = q_weight.shape[2] // head_dim
    kv_heads = vision_kv.shape[3] // (2 * head_dim)
    kv_dev = max(1, kv_heads // n_tensor)
    group = heads_dev // kv_dev
    micro = images.shape[0] // n_replica
    row_count = hidden.shape[1]
    text_len = row_count // micro
    slot_rows = vision_kv.shape[2]
    vis_len = slot_rows * n_tensor * n_section * n_replica
    rows_of_weight = q_weight[0]
    raw = jnp.dot(
        lax.all_gather(hidden, "tensor", axis=2, tiled=True)[0],
        rows_of_weight,
        preferred_element_type=jnp.float32,
    )
    queries = normalize(raw.reshape(row_count, heads_dev, head_dim), q_gain[0]).astype(jnp.bfloat16)
    slots = jnp.arange(vis_len, dtype=jnp.int32)
    within = slots % slot_rows
    rest = slots // slot_rows
    sendbuf = spread(vision_kv, kv_heads, n_tensor, head_dim)
    moved = lax.all_to_all(sendbuf, "tensor", split_axis=3, concat_axis=2, tiled=True)
    moved = moved.reshape(moved.shape[0], moved.shape[1], moved.shape[2], moved.shape[4])
    keyvals = lax.all_to_all(
        lax.all_to_all(moved, "dp", split_axis=1, concat_axis=2, tiled=True),
        "section",
        split_axis=0,
        concat_axis=2,
        tiled=True,
    )
    tensor_of = rest % n_tensor
    rest = rest // n_tensor
    replica_of = rest % n_replica
    section_of = rest // n_replica
    position = ((replica_of * n_section + section_of) * n_tensor + tensor_of) * slot_rows + within
    first_sample = lax.axis_index("dp") * micro
    images_loc = lax.dynamic_slice_in_dim(images, first_sample, micro, 0)
    tiles_loc = lax.dynamic_slice_in_dim(tiles, first_sample, micro, 0)
    start_loc = lax.dynamic_slice_in_dim(text_start, first_sample, micro, 0)
    image_of = position // (TILES * P_SIZE)
    tile_of = position // P_SIZE % TILES
    onehot = (image_of[None, :] == jnp.arange(IMG, dtype=jnp.int32)[:, None]).astype(jnp.int32)
    tile_limit = jnp.sum(tiles_loc[:, :, None] * onehot[None], axis=1)
    first_row = jnp.sum(start_loc[:, :, None] * onehot[None], axis=1)
    live = (image_of[None, :] < images_loc[:, None]) & (tile_of[None, :] < tile_limit)
    text_rows = jnp.arange(text_len, dtype=jnp.int32)
    mask = live[:, None, :] & (text_rows[None, :, None] >= first_row[:, None, :])
    query_heads = queries.reshape(micro, text_len, kv_dev, group, head_dim)
    pairs = keyvals.reshape(micro, vis_len, kv_dev, 2, head_dim)
    keys = normalize(pairs[:, :, :, 0, :].astype(jnp.float32), k_gain[0]).astype(jnp.bfloat16)
    values = pairs[:, :, :, 1, :]
    scores = jnp.einsum(
        "mtkgd,mvkd->mkgtv", query_heads, keys, preferred_element_type=jnp.float32
    ) * head_dim ** (-0.5)
    seen = mask[:, None, None]
    top = jnp.max(jnp.where(seen, scores, -1e30), axis=-1, keepdims=True)
    expo = jnp.where(seen, jnp.exp(scores - top), 0.0)
    total = jnp.maximum(jnp.sum(expo, axis=-1, keepdims=True), 1.0)
    weights = (expo / total).astype(jnp.bfloat16)
    mixed = jnp.einsum(
        "mkgtv,mvkd->mtkgd", weights, values, preferred_element_type=jnp.float32
    ).astype(jnp.bfloat16)
    mixed = mixed.reshape(row_count, heads_dev * head_dim)
    columns = o_weight[0]
    branch = lax.psum_scatter(
        jnp.dot(mixed, columns, preferred_element_type=jnp.float32).T.astype(jnp.bfloat16),
        "tensor",
        scatter_dimension=0,
        tiled=True,
    ).astype(jnp.float32)
    result = hidden[0].astype(jnp.float32) + jnp.tanh(attn_gate[0]) * branch.T
    return result.astype(jnp.bfloat16)[None]


def solution(mesh):
    return jax.shard_map(
        on_device,
        mesh=mesh,
        in_specs=(
            P("section", "dp", "tensor"),
            P("section", None, "tensor"),
            P("section", "tensor", None),
            P(None, None, ("dp", "section", "tensor"), None),
            P("section", None),
            P("section", None),
            P("section"),
            P(),
            P(),
            P(),
        ),
        out_specs=P("section", "dp", "tensor"),
        check_vma=False,
    )
```

profile of v0, /device:TPU:6, one launch (start us, length us, event | category | flops | bytes accessed | tf_op | source)
XLA Modules:
  0.0 374.9 jit_solution(9669682017191379656)
XLA Ops:
  6.5 1.0 copy.49
  7.6 1.1 broadcast_in_dim.25
  8.6 28.7 %all-to-all-start = ((bf16[8,8,1,32,256]{4,1,0,2,3:T(8,128)(2,1)}), bf16[8,8,1,32,256]{4,1,0,2,3:T(8,128)(2,1)S(1)}, u32[]{:S(2)}, u32[]{:S(2)}) async-start(bf16[8,8,1,32,256]{4,1,0,2,3:T(8,128)(2,1)} %bitcast.3), calls=%async_computation | async-start | bytes 2097152 | tf_op jit(solution)/shard_map/all_to_all | solution.py:48
  37.4 0.7 all-gather.2.cloned.1.call-update
  38.1 107.7 %all-to-all-done = bf16[8,8,1,32,256]{4,1,0,2,3:T(8,128)(2,1)S(1)} async-done(((bf16[8,8,1,32,256]{4,1,0,2,3:T(8,128)(2,1)}), bf16[8,8,1,32,256]{4,1,0,2,3:T(8,128)(2,1)S(1)}, u32[]{:S(2)}, u32[]{:S(2)}) %all-to-all-start) | async-done | bytes 1048608 | tf_op jit(solution)/shard_map/all_to_all | solution.py:48
  145.8 1.6 copy.50
  147.4 4.6 %all-to-all-start.1 = ((bf16[8,8,32,256]{3,2,0,1:T(8,128)(2,1)}), bf16[8,8,32,256]{3,2,0,1:T(8,128)(2,1)S(1)}, u32[]{:S(2)}, u32[]{:S(2)}) async-start(bf16[8,8,32,256]{3,2,0,1:T(8,128)(2,1)} %copy.50), calls=%async_computation.1 | async-start | bytes 2097152 | tf_op jit(solution)/shard_map/all_to_all | solution.py:51
  152.0 0.1 constant_dynamic-slice_fusion
  152.1 0.1 copy.47
  152.1 0.1 copy.48
  152.2 0.1 dynamic_slice.9
  152.4 0.1 multiply_reduce_fusion.2
  152.5 0.1 compare_and_fusion
  152.6 14.2 %all-to-all-done.1 = bf16[8,8,32,256]{3,2,0,1:T(8,128)(2,1)S(1)} async-done(((bf16[8,8,32,256]{3,2,0,1:T(8,128)(2,1)}), bf16[8,8,32,256]{3,2,0,1:T(8,128)(2,1)S(1)}, u32[]{:S(2)}, u32[]{:S(2)}) %all-to-all-start.1) | async-done | bytes 1048608 | tf_op jit(solution)/shard_map/all_to_all | solution.py:51
  166.8 1.1 copy.52
  167.9 4.8 %all-to-all-start.2 = ((bf16[8,2,128,256]{3,2,1,0:T(8,128)(2,1)}), bf16[8,2,128,256]{3,2,1,0:T(8,128)(2,1)S(1)}, u32[]{:S(2)}, u32[]{:S(2)}) async-start(bf16[8,2,128,256]{3,2,1,0:T(8,128)(2,1)} %bitcast.8), calls=%async_computation.2 | async-start | bytes 2097152 | tf_op jit(solution)/shard_map/all_to_all | solution.py:50
  172.6 0.1 fusion.16
  172.7 6.4 %copy.64 = bf16[256,8192]{1,0:T(8,128)(2,1)} copy(bf16[256,8192]{0,1:T(8,128)(2,1)} %bitcast.91) | data formatting | bytes 8388608 | tf_op jit(solution)/shard_map/dot_general | solution.py:38
  179.1 50.1 %all-gather.2.cloned.1.call-done = bf16[1,128,8192]{2,1,0:T(8,128)(2,1)} async-done(((bf16[1,128,256]{2,1,0:T(8,128)(2,1)}), bf16[1,128,8192]{2,1,0:T(8,128)(2,1)}) %all-gather.2.cloned.1.call-update) | async-done | bytes 2097168 | tf_op jit(solution)/shard_map/all_gather | solution.py:39
  229.2 4.4 %multiply_reduce_fusion = (f32[128,2]{0,1:T(2,128)S(1)}, f32[128,2,128]{2,0,1:T(8,128)S(1)}) fusion(bf16[2,128,8192]{2,1,0:T(8,128)(2,1)} %bitcast.90, bf16[1,128,8192]{2,1,0:T(8,128)(2,1)} %all-gather.2.cloned.1.call-done), kind=kOutput, calls=%fused_computation.31 | convolution fusion | flops 536936192 | bytes 6423552 | tf_op jit(solution)/shard_map/dot_general | solution.py:38
  233.7 0.1 multiply_convert_fusion
  233.8 0.8 copy.53
  234.6 0.5 reshape.268
  235.1 0.1 fusion.9
  235.2 0.5 select_reduce_fusion
  235.7 0.4 fusion.10
  236.1 0.5 fusion.5
  236.5 0.1 copy.58
  236.6 0.8 copy-done
  237.4 2.1 fusion
  240.2 126.4 %reduce-scatter.2.cloned.1.call-done = bf16[256,128]{0,1:T(8,128)(2,1)} async-done(((bf16[8192,128]{0,1:T(8,128)(2,1)}), bf16[256,128]{0,1:T(8,128)(2,1)}) %reduce-scatter.2.cloned.1.call-update) | async-done | bytes 65552 | tf_op jit(solution)/shard_map/reduce_scatter | solution.py:91
  366.6 1.5 fusion.20
  (22 shorter events, 0.1 us)
Async XLA Ops:
  6.5 145.4 %copy-start.3 = (s32[8,2]{0,1:T(2,128)S(1)}, s32[8,2]{0,1:T(2,128)}, u32[]{:S(2)}) copy-start(s32[8,2]{0,1:T(2,128)} %param.18) | copy-start | bytes 196
  6.5 145.4 %copy-start.2 = (s32[8,2]{0,1:T(2,128)S(1)}, s32[8,2]{0,1:T(2,128)}, u32[]{:S(2)}) copy-start(s32[8,2]{0,1:T(2,128)} %param.19) | copy-start | bytes 196
  6.5 145.7 %copy-start.5 = (s32[8]{0:T(128)S(1)}, s32[8]{0:T(128)}, u32[]{:S(2)}) copy-start(s32[8]{0:T(128)} %param.17) | copy-start | bytes 100
  8.6 137.2 %all-to-all-start = ((bf16[8,8,1,32,256]{4,1,0,2,3:T(8,128)(2,1)}), bf16[8,8,1,32,256]{4,1,0,2,3:T(8,128)(2,1)S(1)}, u32[]{:S(2)}, u32[]{:S(2)}) async-start(bf16[8,8,1,32,256]{4,1,0,2,3:T(8,128)(2,1)} %bitcast.3), calls=%async_computation | async-start | bytes 2097152 | tf_op jit(solution)/shard_map/all_to_all | solution.py:48
  37.4 191.8 %all-gather.2.cloned.1.call-start = ((), (), s32[]{:S(2)}) async-start(), calls=%async_computation.4 | async-start | bytes 2162688 | tf_op jit(solution)/shard_map/all_gather | solution.py:39
  147.4 19.4 %all-to-all-start.1 = ((bf16[8,8,32,256]{3,2,0,1:T(8,128)(2,1)}), bf16[8,8,32,256]{3,2,0,1:T(8,128)(2,1)S(1)}, u32[]{:S(2)}, u32[]{:S(2)}) async-start(bf16[8,8,32,256]{3,2,0,1:T(8,128)(2,1)} %copy.50), calls=%async_computation.1 | async-start | bytes 2097152 | tf_op jit(solution)/shard_map/all_to_all | solution.py:51
  167.9 65.9 %all-to-all-start.2 = ((bf16[8,2,128,256]{3,2,1,0:T(8,128)(2,1)}), bf16[8,2,128,256]{3,2,1,0:T(8,128)(2,1)S(1)}, u32[]{:S(2)}, u32[]{:S(2)}) async-start(bf16[8,2,128,256]{3,2,1,0:T(8,128)(2,1)} %bitcast.8), calls=%async_computation.2 | async-start | bytes 2097152 | tf_op jit(solution)/shard_map/all_to_all | solution.py:50
  172.6 194.0 %reduce-scatter.2.cloned.1.call-start = ((), (), s32[]{:S(2)}) async-start(), calls=%async_computation.5 | async-start | bytes 2162688 | tf_op jit(solution)/shard_map/reduce_scatter | solution.py:91
  179.1 54.5 %copy-start.4 = (f32[1,128]{1,0:T(1,128)S(1)}, f32[1,128]{1,0:T(1,128)}, u32[]{:S(2)}) copy-start(f32[1,128]{1,0:T(1,128)} %param.14) | copy-start | bytes 1540
  229.2 6.0 %copy-start.6 = (f32[1,128]{1,0:T(1,128)S(1)}, f32[1,128]{1,0:T(1,128)}, u32[]{:S(2)}) copy-start(f32[1,128]{1,0:T(1,128)} %param.15) | copy-start | bytes 1540
  235.2 2.2 copy-start
  237.4 129.2 %copy-start.1 = (bf16[1,128,256]{2,1,0:T(8,128)(2,1)S(1)}, bf16[1,128,256]{2,1,0:T(8,128)(2,1)}, u32[]{:S(2)}) copy-start(bf16[1,128,256]{2,1,0:T(8,128)(2,1)} %param.10) | copy-start | bytes 196612
Sparse Core Ops, SparseCore 0:
  40.8 188.3 all-gather.1
  239.6 126.9 reduce-scatter.1
where the time goes:
time: 376 us; the launch traced here: 375 us
  waiting for transfers between devices  299 us (80%)
  starting transfers between devices  38.1 us (10%)
  between operations  14.2 us (4%)
  local copies, waits for them, and re-layouts  13.6 us (4%)
  matrix products  7.41 us (2%)
    reduce_scatter x1, waiting for transfers between devices, on_device(): lax.psum_scatter(jnp.dot(mixed, columns, preferred_element_type=jnp.float...  126 us
    all_to_all x1, waiting for transfers between devices, on_device(): lax.all_to_all(sendbuf, 'tensor', split_axis=3, concat_axis=2, tiled=True)  108 us
    all_gather x1, waiting for transfers between devices, on_device(): lax.all_gather(hidden, 'tensor', axis=2, tiled=True)[0]  50.1 us
    all_to_all x1, starting transfers between devices, on_device(): lax.all_to_all(sendbuf, 'tensor', split_axis=3, concat_axis=2, tiled=True)  28.7 us
    all_to_all x1, waiting for transfers between devices, on_device(): lax.all_to_all(moved, 'dp', split_axis=1, concat_axis=2, tiled=True)  14.2 us
  transfers between devices with their start and end apart: 5, of which 4 were waited for; matrix products, arithmetic and copies ran while one was open for 4% of the time, Pallas kernels for 0%

commit v1 on v0

v1 whole, which is shorter than its diff:
```python
import functools

import jax
import jax.numpy as jnp
from jax import lax
from jax.experimental import pallas as pl
from jax.experimental.pallas import tpu as pltpu
from jax.sharding import PartitionSpec as P

TILES = 4
P_SIZE = 128
MESH = pl.DeviceIdType.MESH
BEFORE_KV = 4


def kernel(
    sizes,
    hidden_ref, kv_ref, qw_hbm, ow_hbm, q_gain_ref, k_gain_ref, gate_ref, images_ref, tiles_ref, start_ref,
    out_ref,
    hid_all, qw, ow, acc, kvx, kv_all, keys, queries, limits, scores, weights, mixed, part,
    got_r, got_l, put_r, put_l,
    local_sem, ag_recv, ag_send_r, ag_send_l, x_recv, x_send, z_recv, z_send, own_send, chain_r, chain_l,
    rs_recv_r, rs_recv_l, rs_send_r, rs_send_l,
):
    n_replica, n_section, n_tensor, kv_heads = sizes
    plane = n_replica * n_section
    group = n_tensor // kv_heads
    reach = (n_tensor - group) // 2
    turn = n_tensor // 2
    rows, width = hidden_ref.shape
    half = rows // 2
    head_dim = width // 2
    block = 2 * plane
    dp = lax.axis_index("dp")
    sec = lax.axis_index("section")
    t = lax.axis_index("tensor")
    me = dp * n_section + sec
    mine = t // group
    j = t % group
    base = mine * group

    def ring(offset):
        return (t + offset + n_tensor) % n_tensor

    right = ring(1)
    left = ring(-1)

    def z_dev(index):
        return (dp, sec, index)

    def plane_dev(index):
        return (index // n_section, index % n_section, t)

    barrier = pltpu.get_barrier_semaphore()

    @pl.loop(1, plane)
    def _(p):
        pl.semaphore_signal(barrier, inc=1, device_id=plane_dev((me + p) % plane), device_id_type=MESH)

    @pl.loop(1, reach + 1)
    def _(p):
        pl.semaphore_signal(barrier, inc=1, device_id=z_dev(ring(p)), device_id_type=MESH)
        pl.semaphore_signal(barrier, inc=1, device_id=z_dev(ring(-p)), device_id_type=MESH)

    qw_copy = pltpu.make_async_copy(qw_hbm, qw, local_sem.at[0])
    ow_copy = pltpu.make_async_copy(ow_hbm, ow, local_sem.at[1])
    qw_copy.start()
    ow_copy.start()
    pl.semaphore_wait(barrier, plane - 1 + 2 * reach)

    def ag_copy(src_ref, source, b, sem, target):
        return pltpu.make_async_remote_copy(
            src_ref=src_ref, dst_ref=hid_all.at[source, b], send_sem=sem, recv_sem=ag_recv.at[source, b],
            device_id=z_dev(target), device_id_type=MESH,
        )

    for b in range(2):
        piece = hidden_ref.at[pl.ds(b * half, half)]
        ag_copy(piece, t, b, ag_send_r.at[0, b], right).start()
        ag_copy(piece, t, b, ag_send_l.at[0, b], left).start()

    def x_copy(peer):
        return pltpu.make_async_remote_copy(
            src_ref=kv_ref.at[peer % n_section, peer // n_section],
            dst_ref=kvx.at[:, pl.ds(2 * me, 2)],
            send_sem=x_send.at[peer], recv_sem=x_recv.at[me],
            device_id=plane_dev(peer), device_id_type=MESH,
        )

    def x_arrival(peer):
        return pltpu.make_async_remote_copy(
            src_ref=kv_ref.at[peer % n_section, peer // n_section],
            dst_ref=kvx.at[:, pl.ds(2 * peer, 2)],
            send_sem=x_send.at[peer], recv_sem=x_recv.at[peer],
            device_id=plane_dev(peer), device_id_type=MESH,
        )

    @pl.loop(1, plane)
    def _(p):
        x_copy((me + p) % plane).start()

    own_x = pltpu.make_async_copy(kv_ref.at[sec, dp], kvx.at[:, pl.ds(2 * me, 2)], local_sem.at[2])
    own_x.start()

    qw_copy.wait()
    acc[...] = jnp.dot(
        hidden_ref[...], qw[pl.ds(pl.multiple_of(t * width, width), width), :], preferred_element_type=jnp.float32
    )

    def project(source):
        chunk = hid_all[source].reshape(rows, width)
        acc[...] += jnp.dot(
            chunk, qw[pl.ds(pl.multiple_of(source * width, width), width), :], preferred_element_type=jnp.float32
        )

    def ag_step(k, carry):
        from_left = ring(-k)
        from_right = ring(k)
        for b in range(2):
            ag_copy(hid_all.at[from_left, b], from_left, b, ag_send_r.at[k, b], right).wait_recv()
            ag_copy(hid_all.at[from_left, b], from_left, b, ag_send_r.at[k, b], right).start()
            ag_copy(hid_all.at[from_right, b], from_right, b, ag_send_l.at[k, b], left).wait_recv()
            ag_copy(hid_all.at[from_right, b], from_right, b, ag_send_l.at[k, b], left).start()
        project(from_left)
        project(from_right)
        return carry

    lax.fori_loop(1, BEFORE_KV, ag_step, 0)

    def z_copy(head, source_ref, source, sem, target):
        del head
        return pltpu.make_async_remote_copy(
            src_ref=source_ref, dst_ref=kv_all.at[source], send_sem=sem, recv_sem=z_recv.at[source],
            device_id=z_dev(target), device_id_type=MESH,
        )

    @pl.loop(1, plane)
    def _(p):
        x_arrival((me + p) % plane).wait_recv()

    own_x.wait()

    def entry(i):
        head = (mine + i) % kv_heads
        ahead = (group * head - t + n_tensor) % n_tensor
        target = group * head + (group - 1) * (ahead // (reach + 1))
        return z_copy(head, kvx.at[pl.ds(2 * head, 2)], t, z_send.at[i], target)

    @pl.loop(1, kv_heads)
    def _(i):
        entry(i).start()

    own_block = kvx.at[pl.ds(2 * mine, 2)]
    own_right = z_copy(mine, own_block, t, own_send.at[0], right)
    own_left = z_copy(mine, own_block, t, own_send.at[1], left)

    @pl.when(j < group - 1)
    def _():
        own_right.start()

    @pl.when(j > 0)
    def _():
        own_left.start()

    own_z = pltpu.make_async_copy(own_block, kv_all.at[t], local_sem.at[3])
    own_z.start()

    lax.fori_loop(BEFORE_KV, turn - 1, ag_step, 0)

    def ag_last(k, to_right, to_left):
        for b in range(2):
            if to_right[b] is not None:
                src = ring(-k)
                ag_copy(hid_all.at[src, b], src, b, ag_send_r.at[k % turn, b], right).wait_recv()
                if to_right[b]:
                    ag_copy(hid_all.at[src, b], src, b, ag_send_r.at[k, b], right).start()
            if to_left[b] is not None:
                src = ring(k)
                ag_copy(hid_all.at[src, b], src, b, ag_send_l.at[k % turn, b], left).wait_recv()
                if to_left[b]:
                    ag_copy(hid_all.at[src, b], src, b, ag_send_l.at[k, b], left).start()

    ag_last(turn - 1, (True, False), (False, True))
    project(ring(1 - turn))
    project(ring(turn - 1))
    ag_last(turn, (False, None), (None, False))
    project(ring(turn))

    for h in range(2):
        raw = acc[:, h * head_dim : (h + 1) * head_dim]
        square = jnp.mean(raw * raw, axis=-1, keepdims=True)
        queries[h * rows : (h + 1) * rows, :] = (raw * lax.rsqrt(square + 1e-05) * q_gain_ref[...]).astype(jnp.bfloat16)

    slots = n_tensor * block
    column = lax.broadcasted_iota(jnp.int32, (1, slots), 1)
    position = (column % block) // 2 * n_tensor + column // block
    image_of = position // (TILES * P_SIZE)
    tile_of = position // P_SIZE % TILES
    for m in range(2):
        sample = dp * 2 + m
        limit = jnp.full((1, slots), half, jnp.int32)
        for image in range(tiles_ref.shape[1]):
            fits = (image_of == image) & (tile_of < tiles_ref[sample, image]) & (image < images_ref[sample])
            limit = jnp.where(fits, start_ref[sample, image], limit)
        limits[m] = jnp.where(column % 2 == m, limit, half)

    def take(source):
        raw = kv_all[source, 0].astype(jnp.float32)
        square = jnp.mean(raw * raw, axis=-1, keepdims=True)
        keys[source] = (raw * lax.rsqrt(square + 1e-05) * k_gain_ref[...]).astype(jnp.bfloat16)

    own_z.wait()
    take(t)

    def chain(n, carry):
        @pl.when(n < reach + j)
        def _():
            src = ring(-1 - n)
            z_copy(mine, kv_all.at[src], src, chain_r.at[n], right).wait_recv()

            @pl.when(j < group - 1)
            def _():
                z_copy(mine, kv_all.at[src], src, chain_r.at[n], right).start()

        @pl.when(n < reach + group - 1 - j)
        def _():
            src = ring(1 + n)
            z_copy(mine, kv_all.at[src], src, chain_l.at[n], left).wait_recv()

            @pl.when(j > 0)
            def _():
                z_copy(mine, kv_all.at[src], src, chain_l.at[n], left).start()

        @pl.when(n < reach + j)
        def _():
            take(ring(-1 - n))

        @pl.when(n < reach + group - 1 - j)
        def _():
            take(ring(1 + n))

        return carry

    lax.fori_loop(0, reach + group - 1, chain, 0)

    scores[...] = lax.dot_general(
        queries[...], keys[...].reshape(slots, head_dim), (((1,), (1,)), ((), ())), preferred_element_type=jnp.float32
    ) * head_dim ** (-0.5)
    step_rows = 16 if half % 16 == 0 else half

    def soften(i, carry):
        r0 = pl.multiple_of(i * step_rows, step_rows)
        m = r0 // half % 2
        text_row = r0 % half + lax.broadcasted_iota(jnp.int32, (step_rows, slots), 0)
        seen = text_row >= limits[m]
        found = jnp.where(seen, scores[pl.ds(r0, step_rows), :], -1e30)
        top = jnp.max(found, axis=-1, keepdims=True)
        expo = jnp.where(seen, jnp.exp(found - top), 0.0)
        total = jnp.maximum(jnp.sum(expo, axis=-1, keepdims=True), 1.0)
        weights[pl.ds(r0, step_rows), :] = (expo / total).astype(jnp.bfloat16)
        return carry

    lax.fori_loop(0, 2 * rows // step_rows, soften, 0)
    both = jnp.dot(
        weights[...], kv_all[:, 1].reshape(slots, head_dim), preferred_element_type=jnp.float32
    ).astype(jnp.bfloat16)
    mixed[:, :head_dim] = both[:rows]
    mixed[:, head_dim:] = both[rows:]

    def share(dest):
        return jnp.dot(
            mixed[...], ow[:, pl.ds(pl.multiple_of(dest * width, width), width)], preferred_element_type=jnp.float32
        )

    def rs_copy(put, got, send, recv, k, b, target):
        return pltpu.make_async_remote_copy(
            src_ref=put.at[k, b], dst_ref=got.at[k, b], send_sem=send.at[k, b], recv_sem=recv.at[k, b],
            device_id=z_dev(target), device_id_type=MESH,
        )

    go_right = functools.partial(rs_copy, put_r, got_r, rs_send_r, rs_recv_r)
    go_left = functools.partial(rs_copy, put_l, got_l, rs_send_l, rs_recv_l)

    ow_copy.wait()
    part[0] = share(ring(turn))
    part[1] = share(ring(1 - turn))
    for b in range(2):
        span = slice(b * half, (b + 1) * half)
        put_r[0, b] = part[0, span].astype(jnp.bfloat16)
        go_right(0, b, right).start()
        put_l[0, b] = part[1, span].astype(jnp.bfloat16)
        go_left(0, b, left).start()
    part[0] = share(ring(turn - 1))
    part[1] = share(ring(2 - turn))

    def rs_step(k, carry):
        for b in range(2):
            span = slice(b * half, (b + 1) * half)
            go_right(k - 1, b, right).wait_recv()
            put_r[k, b] = (got_r[k - 1, b].astype(jnp.float32) + part[0, span]).astype(jnp.bfloat16)
            go_right(k, b, right).start()
            go_left(k - 1, b, left).wait_recv()
            put_l[k, b] = (got_l[k - 1, b].astype(jnp.float32) + part[1, span]).astype(jnp.bfloat16)
            go_left(k, b, left).start()
        part[0] = share(ring(turn - 1 - k))
        part[1] = share(ring(k + 2 - turn))
        return carry

    lax.fori_loop(1, turn - 1, rs_step, 0)
    last = turn - 1
    scale = jnp.tanh(jnp.full((1, width), gate_ref[0], jnp.float32))
    for b in range(2):
        span = slice(b * half, (b + 1) * half)
        go_right(last - 1, b, right).wait_recv()
        put_r[last, b] = (got_r[last - 1, b].astype(jnp.float32) + part[0, span]).astype(jnp.bfloat16)
        go_right(last, b, right).start()
    for b in range(2):
        span = slice(b * half, (b + 1) * half)
        go_left(last - 1, b, left).wait_recv()
        part[1, span] += got_l[last - 1, b].astype(jnp.float32)
    for b in range(2):
        span = slice(b * half, (b + 1) * half)
        go_right(last, b, right).wait_recv()
        total = part[1, span] + got_r[last, b].astype(jnp.float32)
        out_ref[span, :] = (hidden_ref[span, :].astype(jnp.float32) + scale * total).astype(jnp.bfloat16)

    @pl.loop(0, turn - 1)
    def _(k):
        for b in range(2):
            ag_copy(hid_all.at[0, b], 0, b, ag_send_r.at[k, b], right).wait_send()
            ag_copy(hid_all.at[0, b], 0, b, ag_send_l.at[k, b], left).wait_send()

    ag_copy(hid_all.at[0, 0], 0, 0, ag_send_r.at[turn - 1, 0], right).wait_send()
    ag_copy(hid_all.at[0, 1], 0, 1, ag_send_l.at[turn - 1, 1], left).wait_send()

    @pl.loop(1, plane)
    def _(p):
        x_copy((me + p) % plane).wait_send()

    @pl.loop(1, kv_heads)
    def _(i):
        entry(i).wait_send()

    @pl.when(j < group - 1)
    def _():
        own_right.wait_send()

        @pl.loop(0, reach + j)
        def _(n):
            z_copy(mine, kv_all.at[0], 0, chain_r.at[n], right).wait_send()

    @pl.when(j > 0)
    def _():
        own_left.wait_send()

        @pl.loop(0, reach + group - 1 - j)
        def _(n):
            z_copy(mine, kv_all.at[0], 0, chain_l.at[n], left).wait_send()

    @pl.loop(0, turn - 1)
    def _(k):
        for b in range(2):
            go_right(k, b, right).wait_send()
            go_left(k, b, left).wait_send()

    for b in range(2):
        go_right(last, b, right).wait_send()


def on_device(
    hidden, q_weight, o_weight, vision_kv, q_gain, k_gain, attn_gate, images, tiles, text_start
):
    n_tensor = lax.axis_size("tensor")
    n_section = lax.axis_size("section")
    n_replica = lax.axis_size("dp")
    plane = n_section * n_replica
    head_dim = q_gain.shape[1]
    kv_heads = vision_kv.shape[3] // (2 * head_dim)
    rows, width = hidden.shape[1:]
    half = rows // 2
    turn = n_tensor // 2
    group = n_tensor // kv_heads
    reach = (n_tensor - group) // 2
    slots = n_tensor * 2 * plane
    kv = vision_kv.reshape(n_section, n_replica, 2, 2 * kv_heads, head_dim).swapaxes(2, 3)
    bf16, f32 = jnp.bfloat16, jnp.float32
    dma = pltpu.SemaphoreType.DMA
    vmem = pl.BlockSpec(memory_space=pltpu.VMEM)
    smem = pl.BlockSpec(memory_space=pltpu.SMEM)
    hbm = pl.BlockSpec(memory_space=pl.ANY)
    out = pl.pallas_call(
        functools.partial(kernel, (n_replica, n_section, n_tensor, kv_heads)),
        out_shape=jax.ShapeDtypeStruct((rows, width), bf16),
        in_specs=[vmem, vmem, hbm, hbm, vmem, vmem, smem, smem, smem, smem],
        out_specs=vmem,
        scratch_shapes=[
            pltpu.VMEM((n_tensor, 2, half, width), bf16),
            pltpu.VMEM(q_weight.shape[1:], bf16),
            pltpu.VMEM(o_weight.shape[1:], bf16),
            pltpu.VMEM((rows, width), f32),
            pltpu.VMEM((2 * kv_heads, 2 * plane, head_dim), bf16),
            pltpu.VMEM((n_tensor, 2, 2 * plane, head_dim), bf16),
            pltpu.VMEM((n_tensor, 2 * plane, head_dim), bf16),
            pltpu.VMEM((2 * rows, head_dim), bf16),
            pltpu.VMEM((2, 1, slots), jnp.int32),
            pltpu.VMEM((2 * rows, slots), f32),
            pltpu.VMEM((2 * rows, slots), bf16),
            pltpu.VMEM((rows, width), bf16),
            pltpu.VMEM((2, rows, width), f32),
            pltpu.VMEM((turn, 2, half, width), bf16),
            pltpu.VMEM((turn - 1, 2, half, width), bf16),
            pltpu.VMEM((turn, 2, half, width), bf16),
            pltpu.VMEM((turn - 1, 2, half, width), bf16),
            dma((4,)),
            dma((n_tensor, 2)),
            dma((turn, 2)),
            dma((turn, 2)),
            dma((plane,)),
            dma((plane,)),
            dma((n_tensor,)),
            dma((kv_heads,)),
            dma((2,)),
            dma((reach + group - 1,)),
            dma((reach + group - 1,)),
            dma((turn, 2)),
            dma((turn - 1, 2)),
            dma((turn, 2)),
            dma((turn - 1, 2)),
        ],
        compiler_params=pltpu.CompilerParams(
            collective_id=0, has_side_effects=True, vmem_limit_bytes=48 * 1024 * 1024
        ),
    )(
        hidden[0], kv, q_weight[0], o_weight[0], q_gain, k_gain, attn_gate, images, tiles, text_start
    )
    return out[None]


def solution(mesh):
    return jax.shard_map(
        on_device,
        mesh=mesh,
        in_specs=(
            P("section", "dp", "tensor"),
            P("section", None, "tensor"),
            P("section", "tensor", None),
            P(None, None, ("dp", "section", "tensor"), None),
            P("section", None),
            P("section", None),
            P("section"),
            P(),
            P(),
            P(),
        ),
        out_specs=P("section", "dp", "tensor"),
        check_vma=False,
    )
```

time: 376 us -> 212 us (0.56)
  waiting for transfers between devices: 299 us -> 0 us
  Pallas kernels: 0 us -> 203 us
  starting transfers between devices: 38.1 us -> 0 us
  between operations: 14.2 us -> 0.69 us
  matrix products: 7.41 us -> 0 us
  local copies, waits for them, and re-layouts: 13.6 us -> 8.34 us
    pallas_call x0 -> x1, Pallas kernels: none -> 203 us  [on_device(): pl.pallas_call(functools.partial(kernel, (n_replica, n_section, n_tensor,...]
    reduce_scatter x1 -> x0, waiting for transfers between devices: 126 us -> none  [on_device(): lax.psum_scatter(jnp.dot(mixed, columns, preferred_element_type=jnp.float...]
    all_to_all x3 -> x0, waiting for transfers between devices: 122 us -> none  [the longest x1 108 us: on_device(): lax.all_to_all(sendbuf, 'tensor', split_axis=3, concat_axis=2, tiled=True)]
    all_gather x1 -> x0, waiting for transfers between devices: 50.1 us -> none  [on_device(): lax.all_gather(hidden, 'tensor', axis=2, tiled=True)[0]]
    all_to_all x3 -> x0, starting transfers between devices: 38.1 us -> none  [the longest x1 28.7 us: on_device(): lax.all_to_all(sendbuf, 'tensor', split_axis=3, concat_axis=2, tiled=True)]
    dot_general x4 -> x0, matrix products: 7.41 us -> none  [the longest x1 4.44 us: on_device(): jnp.dot(lax.all_gather(hidden, 'tensor', axis=2, tiled=True)[0], rows_of_...]
    unnamed x14, local copies, waits for them, and re-layouts: 0.81 us -> 8.11 us
    dot_general x1 -> x0, local copies, waits for them, and re-layouts: 6.39 us -> none  [on_device(): jnp.dot(lax.all_gather(hidden, 'tensor', axis=2, tiled=True)[0], rows_of_...]
  transfers between devices with their start and end apart: 5 -> 0, of which waited for: 4 -> 0; matrix products, arithmetic and copies ran while one was open for 4% -> 0% of each run, Pallas kernels for 0% -> 0%
where the time goes in v1:
time: 212 us
  Pallas kernels  203 us (96%)
  local copies, waits for them, and re-layouts  8.34 us (4%)
    pallas_call x1, Pallas kernels, on_device(): pl.pallas_call(functools.partial(kernel, (n_replica, n_section, n_tensor,...  203 us
    unnamed x14, local copies, waits for them, and re-layouts  8.11 us

profile of v1, /device:TPU:6, one launch (start us, length us, event | category | flops | bytes accessed | tf_op | source)
XLA Modules:
  0.0 211.8 jit_solution(11671532898602301979)
XLA Ops:
  0.0 1.0 copy.16
  1.0 0.2 copy.18
  1.2 0.8 copy.14.tiles_ref
  2.0 0.8 copy.15.start_ref
  3.4 0.0 copy-start
  3.4 2.2 %copy-done = bf16[1,8192,256]{2,1,0:T(8,128)(2,1)S(1)} copy-done((bf16[1,8192,256]{2,1,0:T(8,128)(2,1)S(1)}, bf16[1,8192,256]{2,1,0:T(8,128)(2,1)}, u32[]{:S(2)}) %copy-start) | copy-done | bytes 4194328
  5.6 0.0 copy-start.1
  5.6 0.8 copy-done.1
  6.4 0.0 copy-start.2
  6.4 0.7 copy-done.2
  7.1 0.0 copy-start.3
  7.1 0.7 copy-done.3
  7.7 0.0 copy-start.4
  7.7 0.7 copy-done.4
  8.4 202.8 %shard_map.100 = bf16[128,256]{1,0:T(8,128)(2,1)S(1)} custom-call(bf16[128,256]{1,0:T(8,128)(2,1)S(1)} %bitcast.16, bf16[8,4,16,2,128]{4,3,2,1,0:T(2,128)(2,1)S(1)} %bitcast.14, bf16[8192,256]{1,0:T(8,128)(2,1)S(1)} %bitcast.13, bf16[256,8192]{1,0:T(8,128)(2,1)} %bitcast.17, f32[1,128]{1,0:T(1,128)S(1)} %copy-done.2, f32[1,128]{1,0:T(1,128)S(1)} %copy-done.3, ...), custom_call_target="tpu_custom_call" | custom-call | tf_op jit(solution)/shard_map/pallas_call | solution.py:391
  211.2 0.6 copy.21
Async XLA Ops:
  3.4 2.2 %copy-start = (bf16[1,8192,256]{2,1,0:T(8,128)(2,1)S(1)}, bf16[1,8192,256]{2,1,0:T(8,128)(2,1)}, u32[]{:S(2)}) copy-start(bf16[1,8192,256]{2,1,0:T(8,128)(2,1)} %param.11) | copy-start | bytes 12582916
  5.6 0.8 copy-start.1
  6.4 0.7 copy-start.2
  7.1 0.7 copy-start.3
  7.7 0.7 copy-start.4

commit v2 on v0

v2 whole, which is shorter than its diff:
```python
import functools

import jax
import jax.numpy as jnp
from jax import lax
from jax.experimental import pallas as pl
from jax.experimental.pallas import tpu as pltpu
from jax.sharding import PartitionSpec as P

TILES = 4
P_SIZE = 128
MESH = pl.DeviceIdType.MESH
EXCHANGED = 3
CHAINED = 6


def kernel(
    sizes,
    hidden_hbm, kv_hbm, qw_hbm, ow_hbm, q_gain_hbm, k_gain_hbm, gate_hbm, images_hbm, tiles_hbm, start_hbm,
    out_ref,
    hid_all, kv_own, qw, ow, q_gain, k_gain, gate, images, tiles, start,
    acc, kvx, kv_all, keys, queries, limits, scores, weights, mixed, part,
    got_r, got_l, put_r, put_l,
    local_sem, kv_sem, ag_recv, ag_send_r, ag_send_l, x_recv, x_send, z_recv, z_send, own_send, chain_r, chain_l,
    rs_recv_r, rs_recv_l, rs_send_r, rs_send_l,
):
    n_replica, n_section, n_tensor, kv_heads = sizes
    plane = n_replica * n_section
    group = n_tensor // kv_heads
    reach = (n_tensor - group) // 2
    turn = n_tensor // 2
    last = turn - 1
    links = reach + group - 1
    rows, width = out_ref.shape
    half = rows // 2
    head_dim = width // 2
    block = 2 * plane
    slots = n_tensor * block
    dp = lax.axis_index("dp")
    sec = lax.axis_index("section")
    t = lax.axis_index("tensor")
    me = dp * n_section + sec
    mine = t // group
    j = t % group

    def ring(offset):
        return (t + offset + n_tensor) % n_tensor

    right = ring(1)
    left = ring(-1)

    def z_dev(index):
        return (dp, sec, index)

    def plane_dev(index):
        return (index // n_section, index % n_section, t)

    barrier = pltpu.get_barrier_semaphore()

    @pl.loop(0, reach)
    def _(p):
        pl.semaphore_signal(barrier, inc=1, device_id=z_dev(ring(reach - p)), device_id_type=MESH)
        pl.semaphore_signal(barrier, inc=1, device_id=z_dev(ring(p - reach)), device_id_type=MESH)

    @pl.loop(1, plane)
    def _(p):
        pl.semaphore_signal(barrier, inc=1, device_id=plane_dev((me + p) % plane), device_id_type=MESH)

    local = [
        pltpu.make_async_copy(src, dst, local_sem.at[i])
        for i, (src, dst) in enumerate([
            (hidden_hbm.at[pl.ds(0, half)], hid_all.at[t, 0]),
            (hidden_hbm.at[pl.ds(half, half)], hid_all.at[t, 1]),
            (qw_hbm, qw),
            (images_hbm, images),
            (tiles_hbm, tiles),
            (start_hbm, start),
            (q_gain_hbm, q_gain),
            (k_gain_hbm, k_gain),
            (gate_hbm, gate),
            (ow_hbm, ow),
        ])
    ]
    columns = [
        pltpu.make_async_copy(
            kv_hbm.at[:, :, pl.ds(i * head_dim, head_dim)], kv_own.at[i], kv_sem.at[i]
        )
        for i in range(2 * kv_heads)
    ]
    for copy in local[:2] + columns + local[2:]:
        copy.start()
    acc[...] = jnp.zeros_like(acc)
    for copy in local[:2] + columns + local[2:]:
        copy.wait()
    pl.semaphore_wait(barrier, plane - 1 + 2 * reach)

    def ag_copy(source, b, sem, target):
        piece = hid_all.at[source, b]
        return pltpu.make_async_remote_copy(
            src_ref=piece, dst_ref=piece, send_sem=sem, recv_sem=ag_recv.at[source, b],
            device_id=z_dev(target), device_id_type=MESH,
        )

    def ag_right(k, b):
        return ag_copy(ring(-k), b, ag_send_r.at[k % turn, b], right)

    def ag_left(k, b):
        return ag_copy(ring(k), b, ag_send_l.at[k % turn, b], left)

    def x_copy(peer, origin):
        return pltpu.make_async_remote_copy(
            src_ref=kv_own.at[:, peer % n_section, pl.ds(2 * (peer // n_section), 2)],
            dst_ref=kvx.at[:, pl.ds(2 * origin, 2)],
            send_sem=x_send.at[peer], recv_sem=x_recv.at[origin],
            device_id=plane_dev(peer), device_id_type=MESH,
        )

    ag_right(0, 0).start()
    ag_left(0, 0).start()

    @pl.loop(1, plane)
    def _(p):
        x_copy((me + p) % plane, me).start()

    own_x = pltpu.make_async_copy(
        kv_own.at[:, sec, pl.ds(2 * dp, 2)], kvx.at[:, pl.ds(2 * me, 2)], local_sem.at[10]
    )
    own_x.start()
    ag_right(0, 1).start()
    ag_left(0, 1).start()

    column = lax.broadcasted_iota(jnp.int32, (1, slots), 1)
    position = (column % block) // 2 * n_tensor + column // block
    image_of = position // (TILES * P_SIZE)
    tile_of = position // P_SIZE % TILES
    for m in range(2):
        sample = dp * 2 + m
        limit = jnp.full((1, slots), half, jnp.int32)
        for image in range(tiles.shape[0]):
            fits = (image_of == image) & (tile_of < tiles[image, sample]) & (image < images[sample])
            limit = jnp.where(fits, start[image, sample], limit)
        limits[m] = jnp.where(column % 2 == m, limit, half)

    def z_copy(source_ref, source, sem, target):
        return pltpu.make_async_remote_copy(
            src_ref=source_ref, dst_ref=kv_all.at[source], send_sem=sem, recv_sem=z_recv.at[source],
            device_id=z_dev(target), device_id_type=MESH,
        )

    def entry(i):
        head = (mine + i) % kv_heads
        ahead = (group * head - t + n_tensor) % n_tensor
        target = group * head + (group - 1) * (ahead // (reach + 1))
        return z_copy(kvx.at[pl.ds(2 * head, 2)], t, z_send.at[i], target)

    def pass_right(n):
        src = ring(-1 - n)
        return z_copy(kv_all.at[src], src, chain_r.at[n], right)

    def pass_left(n):
        src = ring(1 + n)
        return z_copy(kv_all.at[src], src, chain_l.at[n], left)

    own_block = kvx.at[pl.ds(2 * mine, 2)]
    own_right = z_copy(own_block, t, own_send.at[0], right)
    own_left = z_copy(own_block, t, own_send.at[1], left)
    own_z = pltpu.make_async_copy(own_block, kv_all.at[t], local_sem.at[11])

    def take(source):
        raw = kv_all[source, 0].astype(jnp.float32)
        square = jnp.mean(raw * raw, axis=-1, keepdims=True)
        keys[source] = (raw * lax.rsqrt(square + 1e-05) * k_gain[...]).astype(jnp.bfloat16)

    def chain(n):
        to_left_end = n < reach + j
        to_right_end = n < links - j

        @pl.when(to_left_end)
        def _():
            pass_right(n).wait_recv()

            @pl.when(j < group - 1)
            def _():
                pass_right(n).start()

        @pl.when(to_right_end)
        def _():
            pass_left(n).wait_recv()

            @pl.when(j > 0)
            def _():
                pass_left(n).start()

        @pl.when(to_left_end)
        def _():
            take(ring(-1 - n))

        @pl.when(to_right_end)
        def _():
            take(ring(1 + n))

    def enter(q):
        entry(q).start()

        @pl.when(2 * q != kv_heads)
        def _():
            entry(kv_heads - q).start()

    def project(source):
        chunk = hid_all[source].reshape(rows, width)
        acc[...] += jnp.dot(
            chunk, qw[pl.ds(pl.multiple_of(source * width, width), width), :], preferred_element_type=jnp.float32
        )

    def ag_step(k, carry):
        ag_right(k, 0).wait_recv()
        ag_right(k, 0).start()
        ag_left(k, 0).wait_recv()
        ag_left(k, 0).start()
        project(ring(1 - k))

        @pl.when(k == EXCHANGED)
        def _():
            @pl.loop(1, plane)
            def _(p):
                peer = (me + p) % plane
                x_copy(peer, peer).wait_recv()

            own_x.wait()
            own_z.start()

            @pl.when(j < group - 1)
            def _():
                own_right.start()

            @pl.when(j > 0)
            def _():
                own_left.start()

        ag_right(k, 1).wait_recv()
        ag_right(k, 1).start()
        ag_left(k, 1).wait_recv()
        ag_left(k, 1).start()

        @pl.when((k >= EXCHANGED) & ((k - EXCHANGED) % 2 == 0) & (k < EXCHANGED + kv_heads))
        def _():
            enter((k - EXCHANGED) // 2 + 1)

        @pl.when(k > 1)
        def _():
            project(ring(k - 1))

        @pl.when(k >= CHAINED)
        def _():
            for n in range(2):
                @pl.when(2 * (k - CHAINED) + n < links)
                def _():
                    chain(2 * (k - CHAINED) + n)

        return carry

    lax.fori_loop(1, last, ag_step, 0)

    ag_right(last, 0).wait_recv()
    ag_right(last, 0).start()
    ag_left(last, 1).wait_recv()
    ag_left(last, 1).start()
    project(ring(1 - last))
    project(ring(last - 1))
    ag_right(last, 1).wait_recv()
    ag_left(last, 0).wait_recv()
    project(ring(-last))
    project(ring(last))

    @pl.loop(2 * max(0, last - CHAINED), links)
    def _(n):
        chain(n)

    own_z.wait()
    take(t)
    ag_right(turn, 0).wait_recv()
    ag_left(turn, 1).wait_recv()
    project(ring(turn))

    for h in range(2):
        raw = acc[:, h * head_dim : (h + 1) * head_dim]
        square = jnp.mean(raw * raw, axis=-1, keepdims=True)
        normal = (raw * lax.rsqrt(square + 1e-05) * q_gain[...]).astype(jnp.bfloat16)
        for m in range(2):
            queries[m, h * half : (h + 1) * half, :] = normal[m * half : (m + 1) * half]

    step_rows = 16 if half % 16 == 0 else half

    def attend(m):
        scores[...] = lax.dot_general(
            queries[m], keys[...].reshape(slots, head_dim), (((1,), (1,)), ((), ())),
            preferred_element_type=jnp.float32,
        ) * head_dim ** (-0.5)

        def soften(i, carry):
            r0 = pl.multiple_of(i * step_rows, step_rows)
            text_row = r0 % half + lax.broadcasted_iota(jnp.int32, (step_rows, slots), 0)
            seen = text_row >= limits[m]
            found = jnp.where(seen, scores[pl.ds(r0, step_rows), :], -1e30)
            top = jnp.max(found, axis=-1, keepdims=True)
            expo = jnp.where(seen, jnp.exp(found - top), 0.0)
            total = jnp.maximum(jnp.sum(expo, axis=-1, keepdims=True), 1.0)
            weights[pl.ds(r0, step_rows), :] = (expo / total).astype(jnp.bfloat16)
            return carry

        lax.fori_loop(0, rows // step_rows, soften, 0)
        both = jnp.dot(
            weights[...], kv_all[:, 1].reshape(slots, head_dim), preferred_element_type=jnp.float32
        ).astype(jnp.bfloat16)
        for h in range(2):
            mixed[m * half : (m + 1) * half, h * head_dim : (h + 1) * head_dim] = both[h * half : (h + 1) * half]

    def share(dest, span):
        return jnp.dot(
            mixed[span, :], ow[:, pl.ds(pl.multiple_of(dest * width, width), width)],
            preferred_element_type=jnp.float32,
        )

    def rs_copy(put, got, send, recv, target, k, b):
        return pltpu.make_async_remote_copy(
            src_ref=put.at[k, b], dst_ref=got.at[k, b], send_sem=send.at[k, b], recv_sem=recv.at[k, b],
            device_id=z_dev(target), device_id_type=MESH,
        )

    go_right = functools.partial(rs_copy, put_r, got_r, rs_send_r, rs_recv_r, right)
    go_left = functools.partial(rs_copy, put_l, got_l, rs_send_l, rs_recv_l, left)
    spans = (slice(0, half), slice(half, rows))
    whole = slice(0, rows)

    for b in range(2):
        attend(b)
        put_r[0, b] = share(ring(turn), spans[b]).astype(jnp.bfloat16)
        go_right(0, b).start()
        put_l[0, b] = share(ring(1 - turn), spans[b]).astype(jnp.bfloat16)
        go_left(0, b).start()
    part[1, 0] = share(ring(turn - 1), whole)
    part[1, 1] = share(ring(2 - turn), whole)

    def sum_right(k, b):
        go_right(k - 1, b).wait_recv()
        put_r[k, b] = (got_r[k - 1, b].astype(jnp.float32) + part[k % 2, 0, spans[b]]).astype(jnp.bfloat16)
        go_right(k, b).start()

    def sum_left(k, b):
        go_left(k - 1, b).wait_recv()
        put_l[k, b] = (got_l[k - 1, b].astype(jnp.float32) + part[k % 2, 1, spans[b]]).astype(jnp.bfloat16)
        go_left(k, b).start()

    def rs_step(k, carry):
        sum_right(k, 0)
        sum_left(k, 0)
        part[(k + 1) % 2, 0] = share(ring(turn - 1 - k), whole)
        sum_right(k, 1)
        sum_left(k, 1)
        part[(k + 1) % 2, 1] = share(ring(k + 2 - turn), whole)
        for b in range(2):
            ag_right(k - 1, b).wait_send()
            ag_left(k - 1, b).wait_send()
            go_right(k - 1, b).wait_send()
            go_left(k - 1, b).wait_send()
        return carry

    lax.fori_loop(1, last, rs_step, 0)
    sum_right(last, 0)
    sum_right(last, 1)

    for b in range(2):
        ag_right(last - 1, b).wait_send()
        ag_left(last - 1, b).wait_send()
        go_right(last - 1, b).wait_send()
        go_left(last - 1, b).wait_send()
    ag_right(last, 0).wait_send()
    ag_left(last, 1).wait_send()

    @pl.loop(1, plane)
    def _(p):
        x_copy((me + p) % plane, me).wait_send()

    @pl.loop(1, kv_heads)
    def _(i):
        entry(i).wait_send()

    @pl.when(j < group - 1)
    def _():
        own_right.wait_send()

        @pl.loop(0, reach + j)
        def _(n):
            pass_right(n).wait_send()

    @pl.when(j > 0)
    def _():
        own_left.wait_send()

        @pl.loop(0, links - j)
        def _(n):
            pass_left(n).wait_send()

    scale = jnp.tanh(jnp.full((1, width), gate[0], jnp.float32))
    for b in range(2):
        go_left(last - 1, b).wait_recv()
        go_right(last, b).wait_recv()
        total = part[last % 2, 1, spans[b]] + got_l[last - 1, b].astype(jnp.float32) + got_r[last, b].astype(jnp.float32)
        out_ref[spans[b], :] = (hid_all[t, b].astype(jnp.float32) + scale * total).astype(jnp.bfloat16)
    for b in range(2):
        go_right(last, b).wait_send()


def on_device(
    hidden, q_weight, o_weight, vision_kv, q_gain, k_gain, attn_gate, images, tiles, text_start
):
    n_tensor = lax.axis_size("tensor")
    n_section = lax.axis_size("section")
    n_replica = lax.axis_size("dp")
    plane = n_section * n_replica
    head_dim = q_gain.shape[1]
    kv_heads = vision_kv.shape[3] // (2 * head_dim)
    rows, width = hidden.shape[1:]
    half = rows // 2
    turn = n_tensor // 2
    group = n_tensor // kv_heads
    reach = (n_tensor - group) // 2
    slots = n_tensor * 2 * plane
    bf16, f32, i32 = jnp.bfloat16, jnp.float32, jnp.int32
    dma = pltpu.SemaphoreType.DMA
    hbm = pl.BlockSpec(memory_space=pltpu.MemorySpace.HBM)
    n_images = tiles.shape[1]
    samples = images.shape[0]
    out = pl.pallas_call(
        functools.partial(kernel, (n_replica, n_section, n_tensor, kv_heads)),
        out_shape=jax.ShapeDtypeStruct((rows, width), bf16),
        in_specs=[hbm] * 10,
        out_specs=pl.BlockSpec(memory_space=pltpu.VMEM),
        scratch_shapes=[
            pltpu.VMEM((n_tensor, 2, half, width), bf16),
            pltpu.VMEM((2 * kv_heads, n_section, 2 * n_replica, head_dim), bf16),
            pltpu.VMEM(q_weight.shape[1:], bf16),
            pltpu.VMEM(o_weight.shape[1:], bf16),
            pltpu.VMEM((1, head_dim), f32),
            pltpu.VMEM((1, head_dim), f32),
            pltpu.SMEM((1,), f32),
            pltpu.SMEM((samples,), i32),
            pltpu.SMEM((n_images, samples), i32),
            pltpu.SMEM((n_images, samples), i32),
            pltpu.VMEM((rows, width), f32),
            pltpu.VMEM((2 * kv_heads, 2 * plane, head_dim), bf16),
            pltpu.VMEM((n_tensor, 2, 2 * plane, head_dim), bf16),
            pltpu.VMEM((n_tensor, 2 * plane, head_dim), bf16),
            pltpu.VMEM((2, rows, head_dim), bf16),
            pltpu.VMEM((2, 1, slots), i32),
            pltpu.VMEM((rows, slots), f32),
            pltpu.VMEM((rows, slots), bf16),
            pltpu.VMEM((rows, width), bf16),
            pltpu.VMEM((2, 2, rows, width), f32),
            pltpu.VMEM((turn, 2, half, width), bf16),
            pltpu.VMEM((turn - 1, 2, half, width), bf16),
            pltpu.VMEM((turn, 2, half, width), bf16),
            pltpu.VMEM((turn - 1, 2, half, width), bf16),
            dma((12,)),
            dma((2 * kv_heads,)),
            dma((n_tensor, 2)),
            dma((turn, 2)),
            dma((turn, 2)),
            dma((plane,)),
            dma((plane,)),
            dma((n_tensor,)),
            dma((kv_heads,)),
            dma((2,)),
            dma((reach + group - 1,)),
            dma((reach + group - 1,)),
            dma((turn, 2)),
            dma((turn - 1, 2)),
            dma((turn, 2)),
            dma((turn - 1, 2)),
        ],
        compiler_params=pltpu.CompilerParams(
            collective_id=0, has_side_effects=True, vmem_limit_bytes=60 * 1024 * 1024
        ),
    )(
        hidden[0], vision_kv[:, :, 0], q_weight[0], o_weight[0], q_gain, k_gain, attn_gate, images, tiles.T, text_start.T
    )
    return out[None]


def solution(mesh):
    return jax.shard_map(
        on_device,
        mesh=mesh,
        in_specs=(
            P("section", "dp", "tensor"),
            P("section", None, "tensor"),
            P("section", "tensor", None),
            P(None, None, ("dp", "section", "tensor"), None),
            P("section", None),
            P("section", None),
            P("section"),
            P(),
            P(),
            P(),
        ),
        out_specs=P("section", "dp", "tensor"),
        check_vma=False,
    )
```

time: 376 us -> 171 us (0.45)
  waiting for transfers between devices: 299 us -> 0 us
  Pallas kernels: 0 us -> 169 us
  starting transfers between devices: 38.1 us -> 0 us
  between operations: 14.2 us -> 0.66 us
  local copies, waits for them, and re-layouts: 13.6 us -> 1.47 us
  matrix products: 7.41 us -> 0 us
    pallas_call x0 -> x1, Pallas kernels: none -> 169 us  [on_device(): pl.pallas_call(functools.partial(kernel, (n_replica, n_section, n_tensor,...]
    reduce_scatter x1 -> x0, waiting for transfers between devices: 126 us -> none  [on_device(): lax.psum_scatter(jnp.dot(mixed, columns, preferred_element_type=jnp.float...]
    all_to_all x3 -> x0, waiting for transfers between devices: 122 us -> none  [the longest x1 108 us: on_device(): lax.all_to_all(sendbuf, 'tensor', split_axis=3, concat_axis=2, tiled=True)]
    all_gather x1 -> x0, waiting for transfers between devices: 50.1 us -> none  [on_device(): lax.all_gather(hidden, 'tensor', axis=2, tiled=True)[0]]
    all_to_all x3 -> x0, starting transfers between devices: 38.1 us -> none  [the longest x1 28.7 us: on_device(): lax.all_to_all(sendbuf, 'tensor', split_axis=3, concat_axis=2, tiled=True)]
    dot_general x4 -> x0, matrix products: 7.41 us -> none  [the longest x1 4.44 us: on_device(): jnp.dot(lax.all_gather(hidden, 'tensor', axis=2, tiled=True)[0], rows_of_...]
    dot_general x1 -> x0, local copies, waits for them, and re-layouts: 6.39 us -> none  [on_device(): jnp.dot(lax.all_gather(hidden, 'tensor', axis=2, tiled=True)[0], rows_of_...]
  transfers between devices with their start and end apart: 5 -> 0, of which waited for: 4 -> 0; matrix products, arithmetic and copies ran while one was open for 4% -> 0% of each run, Pallas kernels for 0% -> 0%
where the time goes in v2:
time: 171 us
  Pallas kernels  169 us (99%)
    pallas_call x1, Pallas kernels, on_device(): pl.pallas_call(functools.partial(kernel, (n_replica, n_section, n_tensor,...  169 us

profile of v2, /device:TPU:6, one launch (start us, length us, event | category | flops | bytes accessed | tf_op | source)
XLA Modules:
  0.0 171.0 jit_solution(8336993353669276473)
XLA Ops:
  0.7 168.9 %shard_map.100 = bf16[128,256]{1,0:T(8,128)(2,1)} custom-call(bf16[128,256]{1,0:T(8,128)(2,1)} %bitcast.11, bf16[8,8,2048]{2,1,0:T(8,128)(2,1)} %bitcast.10, bf16[8192,256]{1,0:T(8,128)(2,1)} %bitcast.7, bf16[256,8192]{1,0:T(8,128)(2,1)} %bitcast.8, f32[1,128]{1,0:T(1,128)} %q_gain_hbm.1, f32[1,128]{1,0:T(1,128)} %k_gain_hbm.1, f32[1]{0:T(128)S(6)} %copy.12.gate_hbm, ...), custom_call_target="tpu_custom_call" | custom-call | tf_op jit(solution)/shard_map/pallas_call | solution.py:434
  169.5 1.5 copy.13

commit v3 on v2

--- a/solution.py
+++ b/solution.py
@@ -10,8 +10,11 @@
 TILES = 4
 P_SIZE = 128
 MESH = pl.DeviceIdType.MESH
+PIECES = 2
 EXCHANGED = 3
-CHAINED = 6
+CHAINED = 5
+BATCH = 3
+LAG = 5
 
 
 def kernel(
@@ -20,9 +23,9 @@
     out_ref,
     hid_all, kv_own, qw, ow, q_gain, k_gain, gate, images, tiles, start,
     acc, kvx, kv_all, keys, queries, limits, scores, weights, mixed, part,
-    got_r, got_l, put_r, put_l,
+    got_r, got_l, put_r, put_l, near_got_r, near_got_l, near_put_r, near_put_l,
     local_sem, kv_sem, ag_recv, ag_send_r, ag_send_l, x_recv, x_send, z_recv, z_send, own_send, chain_r, chain_l,
-    rs_recv_r, rs_recv_l, rs_send_r, rs_send_l,
+    rs_recv_r, rs_recv_l, rs_send_r, rs_send_l, near_recv_r, near_recv_l, near_send_r, near_send_l,
 ):
     n_replica, n_section, n_tensor, kv_heads = sizes
     plane = n_replica * n_section
@@ -30,9 +33,9 @@
     reach = (n_tensor - group) // 2
     turn = n_tensor // 2
     last = turn - 1
-    links = reach + group - 1
     rows, width = out_ref.shape
     half = rows // 2
+    piece = rows // PIECES
     head_dim = width // 2
     block = 2 * plane
     slots = n_tensor * block
@@ -42,6 +45,7 @@
     me = dp * n_section + sec
     mine = t // group
     j = t % group
+    base = mine * group
 
     def ring(offset):
         return (t + offset + n_tensor) % n_tensor
@@ -69,8 +73,7 @@
     local = [
         pltpu.make_async_copy(src, dst, local_sem.at[i])
         for i, (src, dst) in enumerate([
-            (hidden_hbm.at[pl.ds(0, half)], hid_all.at[t, 0]),
-            (hidden_hbm.at[pl.ds(half, half)], hid_all.at[t, 1]),
+            *((hidden_hbm.at[pl.ds(b * piece, piece)], hid_all.at[t, b]) for b in range(PIECES)),
             (qw_hbm, qw),
             (images_hbm, images),
             (tiles_hbm, tiles),
@@ -87,17 +90,17 @@
         )
         for i in range(2 * kv_heads)
     ]
-    for copy in local[:2] + columns + local[2:]:
+    for copy in local[:PIECES] + columns + local[PIECES:]:
         copy.start()
     acc[...] = jnp.zeros_like(acc)
-    for copy in local[:2] + columns + local[2:]:
+    for copy in local[:PIECES] + columns + local[PIECES:]:
         copy.wait()
     pl.semaphore_wait(barrier, plane - 1 + 2 * reach)
 
     def ag_copy(source, b, sem, target):
-        piece = hid_all.at[source, b]
+        place = hid_all.at[source, b]
         return pltpu.make_async_remote_copy(
-            src_ref=piece, dst_ref=piece, send_sem=sem, recv_sem=ag_recv.at[source, b],
+            src_ref=place, dst_ref=place, send_sem=sem, recv_sem=ag_recv.at[source, b],
             device_id=z_dev(target), device_id_type=MESH,
         )
 
@@ -115,19 +118,19 @@
             device_id=plane_dev(peer), device_id_type=MESH,
         )
 
-    ag_right(0, 0).start()
-    ag_left(0, 0).start()
-
-    @pl.loop(1, plane)
-    def _(p):
-        x_copy((me + p) % plane, me).start()
-
     own_x = pltpu.make_async_copy(
-        kv_own.at[:, sec, pl.ds(2 * dp, 2)], kvx.at[:, pl.ds(2 * me, 2)], local_sem.at[10]
+        kv_own.at[:, sec, pl.ds(2 * dp, 2)], kvx.at[:, pl.ds(2 * me, 2)], local_sem.at[-2 + local_sem.shape[0]]
     )
     own_x.start()
-    ag_right(0, 1).start()
-    ag_left(0, 1).start()
+    for b in range(PIECES):
+        ag_right(0, b).start()
+        ag_left(0, b).start()
+
+        @pl.loop(b * plane // PIECES, (b + 1) * plane // PIECES)
+        def _(p):
+            @pl.when(p > 0)
+            def _():
+                x_copy((me + p) % plane, me).start()
 
     column = lax.broadcasted_iota(jnp.int32, (1, slots), 1)
     position = (column % block) // 2 * n_tensor + column // block
@@ -153,51 +156,51 @@
         target = group * head + (group - 1) * (ahead // (reach + 1))
         return z_copy(kvx.at[pl.ds(2 * head, 2)], t, z_send.at[i], target)
 
-    def pass_right(n):
-        src = ring(-1 - n)
-        return z_copy(kv_all.at[src], src, chain_r.at[n], right)
-
-    def pass_left(n):
-        src = ring(1 + n)
-        return z_copy(kv_all.at[src], src, chain_l.at[n], left)
+    def pass_right(i):
+        src = (base - i + n_tensor) % n_tensor
+        return z_copy(kv_all.at[src], src, chain_r.at[i + group - 2], right)
+
+    def pass_left(i):
+        src = (base + group - 1 + i) % n_tensor
+        return z_copy(kv_all.at[src], src, chain_l.at[i + group - 2], left)
 
     own_block = kvx.at[pl.ds(2 * mine, 2)]
     own_right = z_copy(own_block, t, own_send.at[0], right)
     own_left = z_copy(own_block, t, own_send.at[1], left)
-    own_z = pltpu.make_async_copy(own_block, kv_all.at[t], local_sem.at[11])
+    own_z = pltpu.make_async_copy(own_block, kv_all.at[t], local_sem.at[-1 + local_sem.shape[0]])
 
     def take(source):
         raw = kv_all[source, 0].astype(jnp.float32)
         square = jnp.mean(raw * raw, axis=-1, keepdims=True)
         keys[source] = (raw * lax.rsqrt(square + 1e-05) * k_gain[...]).astype(jnp.bfloat16)
 
+    turns = reach + LAG * (group - 1)
+
     def chain(n):
-        to_left_end = n < reach + j
-        to_right_end = n < links - j
-
-        @pl.when(to_left_end)
-        def _():
-            pass_right(n).wait_recv()
+        i_right = n - LAG * j
+        i_left = n - LAG * (group - 1 - j)
+        to_right = (i_right > -j) & (i_right <= reach)
+        to_left = (i_left > j - group + 1) & (i_left <= reach)
+
+        @pl.when(to_right)
+        def _():
+            pass_right(i_right).wait_recv()
 
             @pl.when(j < group - 1)
             def _():
-                pass_right(n).start()
-
-        @pl.when(to_right_end)
-        def _():
-            pass_left(n).wait_recv()
+                pass_right(i_right).start()
+
+            take((base - i_right + n_tensor) % n_tensor)
+
+        @pl.when(to_left)
+        def _():
+            pass_left(i_left).wait_recv()
 
             @pl.when(j > 0)
             def _():
-                pass_left(n).start()
-
-        @pl.when(to_left_end)
-        def _():
-            take(ring(-1 - n))
-
-        @pl.when(to_right_end)
-        def _():
-            take(ring(1 + n))
+                pass_left(i_left).start()
+
+            take((base + group - 1 + i_left) % n_tensor)
 
     def enter(q):
         entry(q).start()
@@ -213,10 +216,14 @@
         )
 
     def ag_step(k, carry):
-        ag_right(k, 0).wait_recv()
-        ag_right(k, 0).start()
-        ag_left(k, 0).wait_recv()
-        ag_left(k, 0).start()
+        def hand_on(b):
+            ag_right(k, b).wait_recv()
+            ag_right(k, b).start()
+            ag_left(k, b).wait_recv()
+            ag_left(k, b).start()
+
+        for b in range(PIECES // 2):
+            hand_on(b)
         project(ring(1 - k))
 
         @pl.when(k == EXCHANGED)
@@ -237,14 +244,12 @@
             def _():
                 own_left.start()
 
-        ag_right(k, 1).wait_recv()
-        ag_right(k, 1).start()
-        ag_left(k, 1).wait_recv()
-        ag_left(k, 1).start()
-
-        @pl.when((k >= EXCHANGED) & ((k - EXCHANGED) % 2 == 0) & (k < EXCHANGED + kv_heads))
-        def _():
-            enter((k - EXCHANGED) // 2 + 1)
+        for b in range(PIECES // 2, PIECES):
+            hand_on(b)
+
+        @pl.when((k >= EXCHANGED) & (k < EXCHANGED + kv_heads // 2))
+        def _():
+            enter(k - EXCHANGED + 1)
 
         @pl.when(k > 1)
         def _():
@@ -252,34 +257,37 @@
 
         @pl.when(k >= CHAINED)
         def _():
-            for n in range(2):
-                @pl.when(2 * (k - CHAINED) + n < links)
-                def _():
-                    chain(2 * (k - CHAINED) + n)
+            @pl.loop(0, BATCH)
+            def _(n):
+                chain(BATCH * (k - CHAINED) + n + 1)
 
         return carry
 
     lax.fori_loop(1, last, ag_step, 0)
 
-    ag_right(last, 0).wait_recv()
-    ag_right(last, 0).start()
-    ag_left(last, 1).wait_recv()
-    ag_left(last, 1).start()
+    middle = PIECES // 2
+    for b in range(middle):
+        ag_right(last, b).wait_recv()
+        ag_right(last, b).start()
+        ag_left(last, middle + b).wait_recv()
+        ag_left(last, middle + b).start()
     project(ring(1 - last))
     project(ring(last - 1))
-    ag_right(last, 1).wait_recv()
-    ag_left(last, 0).wait_recv()
+    for b in range(middle):
+        ag_right(last, middle + b).wait_recv()
+        ag_left(last, b).wait_recv()
     project(ring(-last))
     project(ring(last))
 
-    @pl.loop(2 * max(0, last - CHAINED), links)
+    @pl.loop(BATCH * max(0, last - CHAINED), turns)
     def _(n):
-        chain(n)
+        chain(n + 1)
 
     own_z.wait()
     take(t)
-    ag_right(turn, 0).wait_recv()
-    ag_left(turn, 1).wait_recv()
+    for b in range(middle):
+        ag_right(turn, b).wait_recv()
+        ag_left(turn, middle + b).wait_recv()
     project(ring(turn))
 
     for h in range(2):
@@ -327,55 +335,94 @@
             device_id=z_dev(target), device_id_type=MESH,
         )
 
-    go_right = functools.partial(rs_copy, put_r, got_r, rs_send_r, rs_recv_r, right)
-    go_left = functools.partial(rs_copy, put_l, got_l, rs_send_l, rs_recv_l, left)
-    spans = (slice(0, half), slice(half, rows))
+    hops = turn // 2
+    go_right = functools.partial(rs_copy, put_r, got_r, rs_send_r, rs_recv_r, ring(2))
+    go_left = functools.partial(rs_copy, put_l, got_l, rs_send_l, rs_recv_l, ring(-2))
+    near_right = functools.partial(rs_copy, near_put_r, near_got_r, near_send_r, near_recv_r, right)
+    near_left = functools.partial(rs_copy, near_put_l, near_got_l, near_send_l, near_recv_l, left)
+    spans = [slice(b * piece, (b + 1) * piece) for b in range(PIECES)]
     whole = slice(0, rows)
 
-    for b in range(2):
-        attend(b)
+    def hand_right(q, b, value):
+        near_put_r[q, b] = value.astype(jnp.bfloat16)
+        near_right(q, b).start()
+
+    def hand_left(q, b, value):
+        near_put_l[q, b] = value.astype(jnp.bfloat16)
+        near_left(q, b).start()
+
+    def sum_right(k, b):
+        near_right(hops - k, b).wait_recv()
+        own = part[k % 2, 0, spans[b]] + near_got_r[hops - k, b].astype(jnp.float32)
+        go_right(k - 1, b).wait_recv()
+        put_r[k, b] = (got_r[k - 1, b].astype(jnp.float32) + own).astype(jnp.bfloat16)
+        go_right(k, b).start()
+
+    def sum_left(k, b):
+        near_left(hops - 1 - k, b).wait_recv()
+        own = part[k % 2, 1, spans[b]] + near_got_l[hops - 1 - k, b].astype(jnp.float32)
+        go_left(k - 1, b).wait_recv()
+        put_l[k, b] = (got_l[k - 1, b].astype(jnp.float32) + own).astype(jnp.bfloat16)
+        go_left(k, b).start()
+
+    for b in range(PIECES):
+        if b * piece % half == 0:
+            attend(b * piece // half)
         put_r[0, b] = share(ring(turn), spans[b]).astype(jnp.bfloat16)
         go_right(0, b).start()
-        put_l[0, b] = share(ring(1 - turn), spans[b]).astype(jnp.bfloat16)
+        hand_left(hops - 1, b, share(ring(1 - turn), spans[b]))
+        hand_right(hops - 1, b, share(ring(turn - 1), spans[b]))
+    part[0, 1] = share(ring(2 - turn), whole)
+    part[1, 0] = share(ring(turn - 2), whole)
+    for b in range(PIECES):
+        near_left(hops - 1, b).wait_recv()
+        put_l[0, b] = (near_got_l[hops - 1, b].astype(jnp.float32) + part[0, 1, spans[b]]).astype(jnp.bfloat16)
         go_left(0, b).start()
-    part[1, 0] = share(ring(turn - 1), whole)
-    part[1, 1] = share(ring(2 - turn), whole)
-
-    def sum_right(k, b):
-        go_right(k - 1, b).wait_recv()
-        put_r[k, b] = (got_r[k - 1, b].astype(jnp.float32) + part[k % 2, 0, spans[b]]).astype(jnp.bfloat16)
-        go_right(k, b).start()
-
-    def sum_left(k, b):
-        go_left(k - 1, b).wait_recv()
-        put_l[k, b] = (got_l[k - 1, b].astype(jnp.float32) + part[k % 2, 1, spans[b]]).astype(jnp.bfloat16)
-        go_left(k, b).start()
+    part[1, 1] = share(ring(4 - turn), whole)
+    early_right = share(ring(turn - 3), whole)
+    early_left = share(ring(3 - turn), whole)
+    for b in range(PIECES):
+        hand_right(hops - 2, b, early_right[spans[b]])
+        hand_left(hops - 2, b, early_left[spans[b]])
 
     def rs_step(k, carry):
-        sum_right(k, 0)
-        sum_left(k, 0)
-        part[(k + 1) % 2, 0] = share(ring(turn - 1 - k), whole)
-        sum_right(k, 1)
-        sum_left(k, 1)
-        part[(k + 1) % 2, 1] = share(ring(k + 2 - turn), whole)
-        for b in range(2):
-            ag_right(k - 1, b).wait_send()
-            ag_left(k - 1, b).wait_send()
+        for b in range(PIECES):
+            sum_right(k, b)
+            sum_left(k, b)
+        q = hops - 2 - k
+        part[(k + 1) % 2, 0] = share(ring(turn - 2 - 2 * k), whole)
+        part[(k + 1) % 2, 1] = share(ring(2 * k + 4 - turn), whole)
+        later_right = share(ring(2 * q + 1), whole)
+        later_left = share(ring(-2 * q - 1), whole)
+        for b in range(PIECES):
+            hand_right(q, b, later_right[spans[b]])
+            hand_left(q, b, later_left[spans[b]])
+        for b in range(PIECES):
+            for n in range(2):
+                ag_right(2 * k - 2 + n, b).wait_send()
+                ag_left(2 * k - 2 + n, b).wait_send()
             go_right(k - 1, b).wait_send()
             go_left(k - 1, b).wait_send()
+            near_right(q + 1, b).wait_send()
+            near_left(q + 1, b).wait_send()
         return carry
 
-    lax.fori_loop(1, last, rs_step, 0)
-    sum_right(last, 0)
-    sum_right(last, 1)
-
-    for b in range(2):
-        ag_right(last - 1, b).wait_send()
-        ag_left(last - 1, b).wait_send()
-        go_right(last - 1, b).wait_send()
-        go_left(last - 1, b).wait_send()
-    ag_right(last, 0).wait_send()
-    ag_left(last, 1).wait_send()
+    lax.fori_loop(1, hops - 1, rs_step, 0)
+    for b in range(PIECES):
+        sum_right(hops - 1, b)
+
+    for b in range(PIECES):
+        for k in range(2 * (hops - 2), last):
+            ag_right(k, b).wait_send()
+            ag_left(k, b).wait_send()
+        go_right(hops - 2, b).wait_send()
+        go_left(hops - 2, b).wait_send()
+        for q in (0, hops - 1):
+            near_right(q, b).wait_send()
+            near_left(q, b).wait_send()
+    for b in range(middle):
+        ag_right(last, b).wait_send()
+        ag_left(last, middle + b).wait_send()
 
     @pl.loop(1, plane)
     def _(p):
@@ -391,24 +438,29 @@
 
         @pl.loop(0, reach + j)
         def _(n):
-            pass_right(n).wait_send()
+            pass_right(reach - n).wait_send()
 
     @pl.when(j > 0)
     def _():
         own_left.wait_send()
 
-        @pl.loop(0, links - j)
+        @pl.loop(0, reach + group - 1 - j)
         def _(n):
-            pass_left(n).wait_send()
+            pass_left(reach - n).wait_send()
 
     scale = jnp.tanh(jnp.full((1, width), gate[0], jnp.float32))
-    for b in range(2):
-        go_left(last - 1, b).wait_recv()
-        go_right(last, b).wait_recv()
-        total = part[last % 2, 1, spans[b]] + got_l[last - 1, b].astype(jnp.float32) + got_r[last, b].astype(jnp.float32)
+    for b in range(PIECES):
+        near_left(0, b).wait_recv()
+        near_right(0, b).wait_recv()
+        total = part[(hops - 1) % 2, 1, spans[b]] + near_got_l[0, b].astype(jnp.float32)
+        total += near_got_r[0, b].astype(jnp.float32)
+        go_left(hops - 2, b).wait_recv()
+        total += got_l[hops - 2, b].astype(jnp.float32)
+        go_right(hops - 1, b).wait_recv()
+        total += got_r[hops - 1, b].astype(jnp.float32)
         out_ref[spans[b], :] = (hid_all[t, b].astype(jnp.float32) + scale * total).astype(jnp.bfloat16)
-    for b in range(2):
-        go_right(last, b).wait_send()
+    for b in range(PIECES):
+        go_right(hops - 1, b).wait_send()
 
 
 def on_device(
@@ -421,8 +473,9 @@
     head_dim = q_gain.shape[1]
     kv_heads = vision_kv.shape[3] // (2 * head_dim)
     rows, width = hidden.shape[1:]
-    half = rows // 2
+    piece = rows // PIECES
     turn = n_tensor // 2
+    hops = turn // 2
     group = n_tensor // kv_heads
     reach = (n_tensor - group) // 2
     slots = n_tensor * 2 * plane
@@ -437,7 +490,7 @@
         in_specs=[hbm] * 10,
         out_specs=pl.BlockSpec(memory_space=pltpu.VMEM),
         scratch_shapes=[
-            pltpu.VMEM((n_tensor, 2, half, width), bf16),
+            pltpu.VMEM((n_tensor, PIECES, piece, width), bf16),
             pltpu.VMEM((2 * kv_heads, n_section, 2 * n_replica, head_dim), bf16),
             pltpu.VMEM(q_weight.shape[1:], bf16),
             pltpu.VMEM(o_weight.shape[1:], bf16),
@@ -457,15 +510,19 @@
             pltpu.VMEM((rows, slots), bf16),
             pltpu.VMEM((rows, width), bf16),
             pltpu.VMEM((2, 2, rows, width), f32),
-            pltpu.VMEM((turn, 2, half, width), bf16),
-            pltpu.VMEM((turn - 1, 2, half, width), bf16),
-            pltpu.VMEM((turn, 2, half, width), bf16),
-            pltpu.VMEM((turn - 1, 2, half, width), bf16),
-            dma((12,)),
+            pltpu.VMEM((hops, PIECES, piece, width), bf16),
+            pltpu.VMEM((hops - 1, PIECES, piece, width), bf16),
+            pltpu.VMEM((hops, PIECES, piece, width), bf16),
+            pltpu.VMEM((hops - 1, PIECES, piece, width), bf16),
+            pltpu.VMEM((hops, PIECES, piece, width), bf16),
+            pltpu.VMEM((hops, PIECES, piece, width), bf16),
+            pltpu.VMEM((hops, PIECES, piece, width), bf16),
+            pltpu.VMEM((hops, PIECES, piece, width), bf16),
+            dma((PIECES + 10,)),
             dma((2 * kv_heads,)),
-            dma((n_tensor, 2)),
-            dma((turn, 2)),
-            dma((turn, 2)),
+            dma((n_tensor, PIECES)),
+            dma((turn, PIECES)),
+            dma((turn, PIECES)),
             dma((plane,)),
             dma((plane,)),
             dma((n_tensor,)),
@@ -473,10 +530,14 @@
             dma((2,)),
             dma((reach + group - 1,)),
             dma((reach + group - 1,)),
-            dma((turn, 2)),
-            dma((turn - 1, 2)),
-            dma((turn, 2)),
-            dma((turn - 1, 2)),
+            dma((hops, PIECES)),
+            dma((hops - 1, PIECES)),
+            dma((hops, PIECES)),
+            dma((hops - 1, PIECES)),
+            dma((hops, PIECES)),
+            dma((hops, PIECES)),
+            dma((hops, PIECES)),
+            dma((hops, PIECES)),
         ],
         compiler_params=pltpu.CompilerParams(
             collective_id=0, has_side_effects=True, vmem_limit_bytes=60 * 1024 * 1024

time: 171 us -> 151 us (0.88)
  Pallas kernels: 169 us -> 148 us
    pallas_call x1, Pallas kernels: 169 us -> 148 us  [on_device(): pl.pallas_call(functools.partial(kernel, (n_replica, n_section, n_tensor,...]
where the time goes in v3:
time: 151 us; the launch traced here: 150 us
  Pallas kernels  148 us (98%)
    pallas_call x1, Pallas kernels, on_device(): pl.pallas_call(functools.partial(kernel, (n_replica, n_section, n_tensor,...  148 us

profile of v3, /device:TPU:6, one launch (start us, length us, event | category | flops | bytes accessed | tf_op | source)
XLA Modules:
  0.0 150.4 jit_solution(4392416321338457827)
XLA Ops:
  0.7 148.3 %shard_map.100 = bf16[128,256]{1,0:T(8,128)(2,1)} custom-call(bf16[128,256]{1,0:T(8,128)(2,1)} %bitcast.11, bf16[8,8,2048]{2,1,0:T(8,128)(2,1)} %bitcast.10, bf16[8192,256]{1,0:T(8,128)(2,1)} %bitcast.7, bf16[256,8192]{1,0:T(8,128)(2,1)} %bitcast.8, f32[1,128]{1,0:T(1,128)} %q_gain_hbm.1, f32[1,128]{1,0:T(1,128)} %k_gain_hbm.1, f32[1]{0:T(128)S(6)} %copy.12.gate_hbm, ...), custom_call_target="tpu_custom_call" | custom-call | tf_op jit(solution)/shard_map/pallas_call | solution.py:487
  149.0 1.5 copy.13
